TPU v7x, 128 devices: a whole 4x4x4 slice. The times are simulated.
128 devices in a mesh: group: 4 (over z_lo, core), dp: 2 (over z_hi), tensor: 16 (over x, y).
Axes of the slice: x: 4, y: 4, z: 4 (z_hi: 2, z_lo: 2; z = z_hi * 2 + z_lo), core: 2. Of those that a mesh axis runs over, the one named last changes fastest.
Arguments:
- tokens: bfloat16 [2048, 8, 2048], P('tensor', ('group', 'dp')), may hold values from -6 to 6
- cotangent: bfloat16 [2048, 8, 2048], P('tensor', ('group', 'dp')), may hold values from -6 to 6
- lengths: int32 [8], replicated, may hold values from 1 to 2048, 9830 in all
- ln1_gain: float32 [2048], replicated, may hold values from 0.25 to 1.75
- ln1_bias: float32 [2048], replicated, may hold values from -1.75 to 1.75
- w_qkv: bfloat16 [2048, 3, 16, 128], P(None, None, 'tensor'), may hold values from -0.125 to 0.125
- b_qv: float32 [2, 2048], P(None, 'tensor'), may hold values from -1.75 to 1.75
- w_o: bfloat16 [16, 128, 2048], P('tensor'), may hold values from -0.75 to 0.75
- b_o: float32 [2048], replicated, may hold values from -1.75 to 1.75
- ln2_gain: float32 [2048], replicated, may hold values from 0.25 to 1.75
- ln2_bias: float32 [2048], replicated, may hold values from -1.75 to 1.75
- w_in: bfloat16 [2048, 8192], P(None, 'tensor'), may hold values from -0.125 to 0.125
- b_in: float32 [8192], P('tensor'), may hold values from -1.75 to 1.75
- w_out: bfloat16 [8192, 2048], P('tensor'), may hold values from -0.0625 to 0.0625
- b_out: float32 [2048], replicated, may hold values from -1.75 to 1.75
Outputs:
- output: bfloat16 [2048, 8, 2048], P('tensor', ('group', 'dp'))
- input_grad: bfloat16 [2048, 8, 2048], P('tensor', ('group', 'dp'))
- d_ln1_gain: float32 [2048], P(('group', 'dp', 'tensor'))
- d_ln1_bias: float32 [2048], P(('group', 'dp', 'tensor'))
- d_w_qkv: float32 [2048, 3, 16, 128], P(('group', 'dp'), None, 'tensor')
- d_b_qv: float32 [2, 2048], P(None, ('group', 'dp', 'tensor'))
- d_w_o: float32 [16, 128, 2048], P('tensor', None, ('group', 'dp'))
- d_b_o: float32 [2048], P(('group', 'dp', 'tensor'))
- d_ln2_gain: float32 [2048], P(('group', 'dp', 'tensor'))
- d_ln2_bias: float32 [2048], P(('group', 'dp', 'tensor'))
- d_w_in: float32 [2048, 8192], P(('group', 'dp'), 'tensor')
- d_b_in: float32 [8192], P(('group', 'dp', 'tensor'))
- d_w_out: float32 [8192, 2048], P('tensor', ('group', 'dp'))
- d_b_out: float32 [2048], P(('group', 'dp', 'tensor'))
Inputs may be any that keep to these rules, and one draw needn't show every extreme that they name: The true lengths of the 8 sequences sum to 9830.
All inputs are finite; a program needn't handle non-finite values.
Results may differ from a plain program's by a relative error of at most 0.02.
Values may be sent and summed in bfloat16 or wider, within the bound.
No kernel may reach another device: no remote copies, remote signals or barrier semaphores. Data moves between devices by JAX's collectives and lax.ppermute only.
A program may use at most 192 MiB of HBM per device.

v0:
```python
from functools import partial
import math
import jax
import jax.numpy as jnp
from jax import lax
from jax.sharding import PartitionSpec as P

EPS = 1e-05
NEGATIVE = -1e30


def layer_norm(value, gain, shift):
    mean = jnp.mean(value, axis=-1, keepdims=True)
    centred = value - mean
    spread = jnp.mean(centred * centred, axis=-1, keepdims=True)
    return centred * lax.rsqrt(spread + EPS) * gain + shift


def gelu_tanh(value):
    return jax.nn.gelu(value, approximate=True)


def block_scores(rows_query, key_rows, first, length, score_scale):
    count = rows_query.shape[0]
    key_pos = jnp.arange(key_rows.shape[0], dtype=jnp.int32)
    query_pos = first + jnp.arange(count, dtype=jnp.int32)
    valid = (key_pos[None, :] <= query_pos[:, None]) & (key_pos[None, :] < length)
    scores = (
        lax.dot_general(
            rows_query, key_rows, (((1,), (1,)), ((), ())), preferred_element_type=jnp.float32
        )
        * score_scale
    )
    return (jnp.where(valid, scores, NEGATIVE), valid)


def attend_forward(item, block_rows, score_scale):
    query, key_rows, value_rows, length = item
    outputs = []
    log_parts = []
    for first in range(0, query.shape[0], block_rows):
        rows_query = query[first : first + block_rows]
        scores, valid = block_scores(rows_query, key_rows, first, length, score_scale)
        peak = jnp.max(scores, axis=-1, keepdims=True)
        expo = jnp.exp(scores - peak)
        weight_sum = jnp.sum(expo, axis=-1, keepdims=True)
        probs = (expo / weight_sum).astype(jnp.bfloat16)
        outputs.append(
            jnp.dot(probs, value_rows, preferred_element_type=jnp.float32).astype(jnp.bfloat16)
        )
        log_parts.append((peak + jnp.log(weight_sum))[:, 0])
    return (jnp.concatenate(outputs, 0), jnp.concatenate(log_parts, 0))


def attend_backward(item, block_rows, score_scale):
    query, key_rows, value_rows, length, grad_out, log_sums = item
    key_grad = jnp.zeros(key_rows.shape, jnp.float32)
    value_grad = jnp.zeros(value_rows.shape, jnp.float32)
    query_parts = []
    for first in range(0, query.shape[0], block_rows):
        rows_query = query[first : first + block_rows]
        scores, valid = block_scores(rows_query, key_rows, first, length, score_scale)
        probs = jnp.where(valid, jnp.exp(scores - log_sums[first : first + block_rows, None]), 0.0)
        grad_rows = grad_out[first : first + block_rows]
        probs_grad = lax.dot_general(
            grad_rows, value_rows, (((1,), (1,)), ((), ())), preferred_element_type=jnp.float32
        )
        inner = jnp.sum(probs * probs_grad, axis=-1, keepdims=True)
        score_grad = (probs * (probs_grad - inner)).astype(jnp.bfloat16)
        query_parts.append(
            jnp.dot(score_grad, key_rows, preferred_element_type=jnp.float32) * score_scale
        )
        key_grad = (
            key_grad
            + lax.dot_general(
                score_grad, rows_query, (((0,), (0,)), ((), ())), preferred_element_type=jnp.float32
            )
            * score_scale
        )
        value_grad = value_grad + lax.dot_general(
            probs.astype(jnp.bfloat16),
            grad_rows,
            (((0,), (0,)), ((), ())),
            preferred_element_type=jnp.float32,
        )
    return (
        jnp.concatenate(query_parts, 0).astype(jnp.bfloat16),
        key_grad.astype(jnp.bfloat16),
        value_grad.astype(jnp.bfloat16),
    )


def shards(
    tokens,
    cotangent,
    lengths,
    ln1_gain,
    ln1_bias,
    w_qkv,
    b_qv,
    w_o,
    b_o,
    ln2_gain,
    ln2_bias,
    w_in,
    b_in,
    w_out,
    b_out,
):
    row_count, seq_count, model_width = tokens.shape
    tensor_count = lax.axis_size("tensor")
    tensor_rank = lax.axis_index("tensor")
    seq_total = row_count * tensor_count
    local_heads = w_qkv.shape[2]
    head_size = w_qkv.shape[3]
    local_width = local_heads * head_size
    hidden = w_in.shape[1]
    block_rows = min(512, seq_total)
    score_scale = 1.0 / math.sqrt(head_size)
    group_count = lax.axis_size("group")
    group_rank = lax.axis_index("group")
    member = group_rank * lax.axis_size("dp") + lax.axis_index("dp")
    seq_lengths = lax.dynamic_slice_in_dim(lengths, member * seq_count, seq_count, 0)
    group_totals = jnp.sum(lengths.reshape(group_count, -1), axis=1).astype(jnp.float32)
    factor = (
        group_count
        * lax.dynamic_index_in_dim(group_totals, group_rank, 0, keepdims=False)
        / jnp.sum(group_totals)
    )
    inputs = tokens.astype(jnp.float32)
    normed_low = layer_norm(inputs, ln1_gain, ln1_bias).astype(jnp.bfloat16)
    normed_full = lax.all_gather(normed_low, "tensor", axis=0, tiled=True)
    joint_weight = w_qkv.reshape(model_width, 3 * local_width)
    projected = jnp.dot(
        normed_full.reshape(seq_total * seq_count, model_width),
        joint_weight,
        preferred_element_type=jnp.float32,
    )
    projected = projected.reshape(seq_total, seq_count, 3, local_width)
    query = (projected[:, :, 0] + b_qv[0]).astype(jnp.bfloat16)
    keys = projected[:, :, 1].astype(jnp.bfloat16)
    values = (projected[:, :, 2] + b_qv[1]).astype(jnp.bfloat16)

    def per_item(array):
        shaped = array.reshape(seq_total, seq_count, local_heads, head_size)
        return jnp.transpose(shaped, (1, 2, 0, 3)).reshape(
            seq_count * local_heads, seq_total, head_size
        )

    def per_row(array):
        shaped = array.reshape(seq_count, local_heads, seq_total, head_size)
        return jnp.transpose(shaped, (2, 0, 1, 3)).reshape(seq_total, seq_count, local_width)

    query_items = per_item(query)
    key_items = per_item(keys)
    value_items = per_item(values)
    item_lengths = jnp.repeat(seq_lengths, local_heads)
    heads_out, log_sums = lax.map(
        partial(attend_forward, block_rows=block_rows, score_scale=score_scale),
        (query_items, key_items, value_items, item_lengths),
    )
    attended = per_row(heads_out)
    out_weight = w_o.reshape(local_width, model_width)
    piece = attended
    attention = (
        lax.psum_scatter(
            jnp.einsum("rse,ed->rsd", piece, out_weight, preferred_element_type=jnp.float32),
            "tensor",
            scatter_dimension=0,
            tiled=True,
        )
        + b_o
    )
    middle = inputs + attention
    second_low = layer_norm(middle, ln2_gain, ln2_bias).astype(jnp.bfloat16)
    second_full = lax.all_gather(second_low, "tensor", axis=0, tiled=True)
    pre_act = (
        jnp.dot(
            second_full.reshape(seq_total * seq_count, model_width),
            w_in,
            preferred_element_type=jnp.float32,
        )
        + b_in
    )
    activated = gelu_tanh(pre_act).astype(jnp.bfloat16).reshape(seq_total, seq_count, hidden)
    piece = activated
    feed = (
        lax.psum_scatter(
            jnp.einsum("rsf,fd->rsd", piece, w_out, preferred_element_type=jnp.float32).astype(
                jnp.bfloat16
            ),
            "tensor",
            scatter_dimension=0,
            tiled=True,
        ).astype(jnp.float32)
        + b_out
    )
    output = (middle + feed).astype(jnp.bfloat16)
    positions = tensor_rank * row_count + jnp.arange(row_count, dtype=jnp.int32)
    live = positions[:, None] < seq_lengths[None, :]
    upstream = jnp.where(live[:, :, None], cotangent, jnp.zeros_like(cotangent))
    piece = lax.all_gather(upstream, "tensor", axis=0, tiled=True)
    weight_grad = jnp.einsum("rsf,rsd->fd", activated, piece, preferred_element_type=jnp.float32)
    part = jnp.einsum("rsd,fd->rsf", piece, w_out, preferred_element_type=jnp.float32)
    act_grad = part
    grad_w_out = weight_grad
    gelu_back = jax.vjp(gelu_tanh, pre_act)[1]
    pre_low = gelu_back(act_grad.reshape(seq_total * seq_count, hidden))[0].astype(jnp.bfloat16)
    grad_b_in = jnp.sum(pre_low, axis=0, dtype=jnp.float32)
    grad_w_in = jnp.einsum(
        "rd,rf->df",
        second_full.reshape(seq_total * seq_count, model_width),
        pre_low,
        preferred_element_type=jnp.float32,
    )
    pre_rows = pre_low.reshape(seq_total, seq_count, hidden)
    piece = pre_rows
    second_grad = lax.psum_scatter(
        jnp.einsum("rsf,df->rsd", piece, w_in, preferred_element_type=jnp.float32),
        "tensor",
        scatter_dimension=0,
        tiled=True,
    )
    norm_two_back = jax.vjp(layer_norm, middle, ln2_gain, ln2_bias)[1]
    middle_part, grad_ln2_gain, grad_ln2_bias = norm_two_back(second_grad)
    middle_grad = upstream.astype(jnp.float32) + middle_part
    branch_low = middle_grad.astype(jnp.bfloat16)
    grad_b_o = jnp.sum(branch_low, axis=(0, 1), dtype=jnp.float32)
    grad_b_out = jnp.sum(upstream, axis=(0, 1), dtype=jnp.float32)
    piece = lax.all_gather(branch_low, "tensor", axis=0, tiled=True)
    weight_grad = jnp.einsum("rse,rsd->ed", attended, piece, preferred_element_type=jnp.float32)
    part = jnp.einsum("rsd,ed->rse", piece, out_weight, preferred_element_type=jnp.float32)
    head_items = per_item(part.astype(jnp.bfloat16))
    grads_query, grads_keys, grads_values = lax.map(
        partial(attend_backward, block_rows=block_rows, score_scale=score_scale),
        (query_items, key_items, value_items, item_lengths, head_items, log_sums),
    )
    joint_grad = jnp.stack(
        (per_row(grads_query), per_row(grads_keys), per_row(grads_values)), axis=2
    )
    grad_b_qv = jnp.sum(joint_grad[:, :, 0::2], axis=(0, 1), dtype=jnp.float32)
    joint_rows = joint_grad.reshape(seq_total, seq_count, 3 * local_width)
    grad_w_qkv = jnp.einsum(
        "rd,rc->dc",
        normed_full.reshape(seq_total * seq_count, model_width),
        joint_rows.reshape(seq_total * seq_count, 3 * local_width),
        preferred_element_type=jnp.float32,
    )
    piece = joint_rows
    normed_grad = lax.psum_scatter(
        jnp.einsum("rsc,dc->rsd", piece, joint_weight, preferred_element_type=jnp.float32).astype(
            jnp.bfloat16
        ),
        "tensor",
        scatter_dimension=0,
        tiled=True,
    ).astype(jnp.float32)
    norm_one_back = jax.vjp(layer_norm, inputs, ln1_gain, ln1_bias)[1]
    input_part, grad_ln1_gain, grad_ln1_bias = norm_one_back(normed_grad)
    input_grad = (middle_grad + input_part).astype(jnp.bfloat16)
    matrices = (
        grad_w_qkv.reshape(model_width, 3, local_heads, head_size) * factor,
        weight_grad.reshape(local_heads, head_size, model_width) * factor,
        grad_w_in * factor,
        grad_w_out * factor,
    )
    summed = (
        lax.psum_scatter(
            matrices[0].astype(jnp.bfloat16), ("group", "dp"), scatter_dimension=0, tiled=True
        ).astype(jnp.float32),
        lax.psum_scatter(
            matrices[1].astype(jnp.bfloat16), ("group", "dp"), scatter_dimension=2, tiled=True
        ).astype(jnp.float32),
        lax.psum_scatter(
            matrices[2].astype(jnp.bfloat16), ("group", "dp"), scatter_dimension=0, tiled=True
        ).astype(jnp.float32),
        lax.psum_scatter(
            matrices[3].astype(jnp.bfloat16), ("group", "dp"), scatter_dimension=1, tiled=True
        ).astype(jnp.float32),
    )
    in_full = lax.dynamic_update_slice_in_dim(
        jnp.zeros((hidden * tensor_count,), jnp.float32), grad_b_in, tensor_rank * hidden, 0
    )
    joint_full = lax.dynamic_update_slice_in_dim(
        jnp.zeros((2, local_width * tensor_count), jnp.float32),
        grad_b_qv,
        tensor_rank * local_width,
        1,
    )
    stacked = (
        jnp.concatenate(
            (
                jnp.stack(
                    (
                        grad_ln1_gain,
                        grad_ln1_bias,
                        grad_b_o,
                        grad_ln2_gain,
                        grad_ln2_bias,
                        grad_b_out,
                    )
                ),
                joint_full,
            ),
            0,
        )
        * factor
    )
    vector_sums, in_sums = (
        lax.psum_scatter(stacked, ("group", "dp", "tensor"), scatter_dimension=1, tiled=True),
        lax.psum_scatter(
            in_full * factor, ("group", "dp", "tensor"), scatter_dimension=0, tiled=True
        ),
    )
    return (
        output,
        input_grad,
        vector_sums[0],
        vector_sums[1],
        summed[0],
        vector_sums[6:8],
        summed[1],
        vector_sums[2],
        vector_sums[3],
        vector_sums[4],
        summed[2],
        in_sums,
        summed[3],
        vector_sums[5],
    )


def solution(mesh):
    in_specs = (
        P("tensor", ("group", "dp"), None),
        P("tensor", ("group", "dp"), None),
        P(),
        P(),
        P(),
        P(None, None, "tensor", None),
        P(None, "tensor"),
        P("tensor", None, None),
        P(),
        P(),
        P(),
        P(None, "tensor"),
        P("tensor"),
        P("tensor", None),
        P(),
    )
    out_specs = (
        P("tensor", ("group", "dp"), None),
        P("tensor", ("group", "dp"), None),
        P(("group", "dp", "tensor")),
        P(("group", "dp", "tensor")),
        P(("group", "dp"), None, "tensor", None),
        P(None, ("group", "dp", "tensor")),
        P("tensor", None, ("group", "dp")),
        P(("group", "dp", "tensor")),
        P(("group", "dp", "tensor")),
        P(("group", "dp", "tensor")),
        P(("group", "dp"), "tensor"),
        P(("group", "dp", "tensor")),
        P("tensor", ("group", "dp")),
        P(("group", "dp", "tensor")),
    )
    return jax.shard_map(shards, mesh=mesh, in_specs=in_specs, out_specs=out_specs, check_vma=False)
```

profile of v0, /device:TPU:96, one launch (start us, length us, event | category | flops | bytes accessed | tf_op | source)
XLA Modules:
  0.0 1723.6 jit_solution(11324964571885417214)
XLA Ops:
  7.3 1.3 convert_reduce_fusion.3
  8.6 1.3 fusion.81
  10.5 2.3 fusion.80
  12.8 2.6 copy.51
  16.8 68.1 %all-gather.5.cloned.1.call-done = bf16[2048,1,2048]{2,0,1:T(8,128)(2,1)} async-done(((bf16[128,1,2048]{2,0,1:T(8,128)(2,1)}), bf16[2048,1,2048]{2,0,1:T(8,128)(2,1)}) %all-gather.5.cloned.1.call-update) | async-done | bytes 8388624 | tf_op jit(solution)/shard_map/all_gather | solution.py:132
  84.8 7.4 fusion.31
  93.6 3.6 fusion.113
  97.1 3.9 fusion.116
  101.0 4.0 online-softmax.3
  106.0 5.1 fusion.115
  111.1 4.0 online-softmax.2
  116.1 5.1 fusion.114
  121.1 4.0 online-softmax.1
  126.2 4.4 online-softmax
  132.2 8.1 convolution_bitcast_fusion.1
  140.4 110.3 %reduce-scatter.12.cloned.1.call-done = f32[128,1,2048]{2,0,1:T(8,128)} async-done(((f32[2048,1,2048]{2,0,1:T(8,128)}), f32[128,1,2048]{2,0,1:T(8,128)}) %reduce-scatter.12.cloned.1.call-update) | async-done | bytes 1048592 | tf_op jit(solution)/shard_map/reduce_scatter | solution.py:166
  250.7 1.6 fusion.111
  253.6 1.7 add_convert_fusion.3
  256.1 2.6 convert_reduce_fusion.4
  258.8 67.0 %all-gather.7.cloned.1.call-done = bf16[2048,1,2048]{2,0,1:T(8,128)(2,1)} async-done(((bf16[128,1,2048]{2,0,1:T(8,128)(2,1)}), bf16[2048,1,2048]{2,0,1:T(8,128)(2,1)}) %all-gather.7.cloned.1.call-update) | async-done | bytes 8388624 | tf_op jit(solution)/shard_map/all_gather | solution.py:176
  325.7 10.5 fusion.10
  336.2 62.4 %all-gather.9.cloned.1.call-done = bf16[2048,1,2048]{2,0,1:T(8,128)(2,1)} async-done(((bf16[128,1,2048]{2,0,1:T(8,128)(2,1)}), bf16[2048,1,2048]{2,0,1:T(8,128)(2,1)}) %all-gather.9.cloned.1.call-update) | async-done | bytes 8388624 | tf_op jit(solution)/shard_map/all_gather | solution.py:202
  398.7 12.4 convert_reduce_fusion
  411.1 1.4 copy-done.72
  412.5 8.2 convolution_bitcast_fusion
  420.8 10.3 convert_bitcast_fusion.1
  431.2 99.9 %reduce-scatter.16.cloned.1.call-done = f32[128,1,2048]{2,0,1:T(8,128)} async-done(((f32[2048,1,2048]{2,0,1:T(8,128)}), f32[128,1,2048]{2,0,1:T(8,128)}) %reduce-scatter.16.cloned.1.call-update) | async-done | bytes 1048592 | tf_op jit(solution)/shard_map/reduce_scatter | solution.py:218
  531.1 2.2 multiply_reduce_fusion.4
  533.3 85.7 %reduce-scatter.14.cloned.1.call-done = bf16[128,1,2048]{2,0,1:T(8,128)(2,1)} async-done(((bf16[2048,1,2048]{2,0,1:T(8,128)(2,1)}), bf16[128,1,2048]{2,0,1:T(8,128)(2,1)}) %reduce-scatter.14.cloned.1.call-update) | async-done | bytes 524304 | tf_op jit(solution)/shard_map/reduce_scatter | solution.py:188
  619.0 2.5 fusion.110
  625.8 11.3 multiply_convert_fusion
  637.2 3.1 exponential_reduce_fusion
  645.5 9.6 multiply_convert_fusion.1
  655.6 37.3 %all-gather.11.cloned.1.call-done = bf16[2048,1,2048]{2,0,1:T(8,128)(2,1)} async-done(((bf16[128,1,2048]{2,0,1:T(8,128)(2,1)}), bf16[2048,1,2048]{2,0,1:T(8,128)(2,1)}) %all-gather.11.cloned.1.call-update) | async-done | bytes 8388624 | tf_op jit(solution)/shard_map/all_gather | solution.py:230
  692.9 5.9 fusion.45
  698.8 2.8 fusion.97
  701.7 2.9 fusion.100
  704.6 2.7 fusion.103
  708.0 9.5 multiply_reduce_fusion
  717.5 4.5 multiply_convert_fusion.3
  722.1 9.5 multiply_convert_fusion.2
  731.6 2.1 fusion.75
  733.7 3.3 fusion.77
  737.0 1.4 fusion.78
  738.4 1.4 fusion.76
  743.7 1.7 convolution_add_fusion.2
  745.5 1.7 convolution_add_fusion.1
  747.2 2.8 fusion.56
  750.0 2.3 fusion.53
  753.6 1.6 copy.60
  755.2 8.3 fusion.38
  763.6 9.7 convert_bitcast_fusion
  774.1 75.9 %all-reduce = f32[8192]{0:T(1024)S(1)} all-reduce(f32[8192]{0:T(1024)S(1)} %broadcast_multiply_fusion.1), channel_id=10, replica_groups=mesh['group'=4,'dp'=2,'tensor'=16] {'group','dp','tensor'}, use_global_device_ids=true, to_apply=%region_38.39.clone | all-reduce | flops 8192 | bytes 65536
  850.6 1.8 convert_element_type.264
  852.4 1.8 convert_element_type.261
  855.4 1.7 convert_element_type.259
  857.0 45.5 %reduce-scatter.20.cloned.1.call-done = bf16[256,3,1,128]{3,0,1,2:T(8,128)(2,1)} async-done(((bf16[2048,3,1,128]{3,0,1,2:T(8,128)(2,1)}), bf16[256,3,1,128]{3,0,1,2:T(8,128)(2,1)}) %reduce-scatter.20.cloned.1.call-update) | async-done | bytes 196624 | tf_op jit(solution)/shard_map/reduce_scatter | solution.py:268
  902.5 2.0 copy.62
  904.5 90.2 %reduce-scatter.18.cloned.1.call-done = bf16[128,1,2048]{2,0,1:T(8,128)(2,1)} async-done(((bf16[2048,1,2048]{2,0,1:T(8,128)(2,1)}), bf16[128,1,2048]{2,0,1:T(8,128)(2,1)}) %reduce-scatter.18.cloned.1.call-update) | async-done | bytes 524304 | tf_op jit(solution)/shard_map/reduce_scatter | solution.py:250
  994.7 1.4 convert_reduce_fusion.2
  996.1 1.6 fusion.83
  997.9 1.3 copy.73
  999.2 2.7 add_convert_fusion
  1002.0 709.0 %reduce-scatter.28.cloned.1.call-done = f32[16,8]{1,0:T(8,128)} async-done(((f32[2048,8]{1,0:T(8,128)}), f32[16,8]{1,0:T(8,128)}) %reduce-scatter.28.cloned.1.call-update) | async-done | bytes 528
  (239 shorter events, 33.2 us)
Async XLA Ops:
  7.2 391.5 %copy-start = (bf16[512,2048]{1,0:T(8,128)(2,1)S(1)}, bf16[512,2048]{1,0:T(8,128)(2,1)}, u32[]{:S(2)}) copy-start(bf16[512,2048]{1,0:T(8,128)(2,1)} %param.28) | copy-start | bytes 6291460
  7.2 8.3 copy-start.66
  7.2 9.5 copy-start.63
  7.2 77.6 %all-gather.5.cloned.1.call-start = ((), (), s32[]{:S(2)}) async-start(), calls=%async_computation.9 | async-start | bytes 8912896 | tf_op jit(solution)/shard_map/all_gather | solution.py:132
  9.9 82.3 %copy-start.68 = (f32[128]{0:T(128)}, f32[128]{0:T(128)S(1)}, u32[]{:S(2)}) copy-start(f32[128]{0:T(128)S(1)} %fusion.81) | copy-start | bytes 1540
  12.8 237.9 %reduce-scatter.12.cloned.1.call-start = ((), (), s32[]{:S(2)}) async-start(), calls=%async_computation.10 | async-start | bytes 17825792 | tf_op jit(solution)/shard_map/reduce_scatter | solution.py:166
  16.0 100.0 %copy-start.35 = (s32[512]{0:T(512)}, s32[512]{0:T(512)S(1)}, u32[]{:S(2)}) copy-start(s32[512]{0:T(512)S(1)} %iota_add_fusion.2) | copy-start | bytes 6148
  16.0 89.9 %copy-start.33 = (s32[512]{0:T(512)}, s32[512]{0:T(512)S(1)}, u32[]{:S(2)}) copy-start(s32[512]{0:T(512)S(1)} %iota_add_fusion.1) | copy-start | bytes 6148
  16.7 75.6 %copy-start.56 = (f32[128]{0:T(128)}, f32[128]{0:T(128)S(1)}, u32[]{:S(2)}) copy-start(f32[128]{0:T(128)S(1)} %get-tuple-element.136) | copy-start | bytes 1540
  92.2 4.9 copy-start.12
  92.3 23.7 %copy-start.17 = (bf16[2048,1,128]{2,0,1:T(8,128)(2,1)}, bf16[2048,1,128]{2,0,1:T(8,128)(2,1)S(1)}, u32[]{:S(2)}) copy-start(bf16[2048,1,128]{2,0,1:T(8,128)(2,1)S(1)} %fusion.85) | copy-start | bytes 1572868
  125.1 7.1 copy-start.23
  140.3 113.3 %copy-start.29 = (f32[2048]{0:T(1024)S(1)}, f32[2048]{0:T(1024)}, u32[]{:S(2)}) copy-start(f32[2048]{0:T(1024)} %param.24) | copy-start | bytes 24580
  140.3 185.4 %all-gather.7.cloned.1.call-start = ((), (), s32[]{:S(2)}) async-start(), calls=%async_computation.11 | async-start | bytes 8912896 | tf_op jit(solution)/shard_map/all_gather | solution.py:176
  255.3 143.3 %all-gather.9.cloned.1.call-start = ((), (), s32[]{:S(2)}) async-start(), calls=%async_computation.13 | async-start | bytes 8912896 | tf_op jit(solution)/shard_map/all_gather | solution.py:202
  258.7 272.4 %reduce-scatter.16.cloned.1.call-start = ((), (), s32[]{:S(2)}) async-start(), calls=%async_computation.14 | async-start | bytes 17825792 | tf_op jit(solution)/shard_map/reduce_scatter | solution.py:218
  398.7 13.8 copy-start.70
  420.7 198.3 %reduce-scatter.14.cloned.1.call-start = ((), (), s32[]{:S(2)}) async-start(), calls=%async_computation.12 | async-start | bytes 8912896 | tf_op jit(solution)/shard_map/reduce_scatter | solution.py:188
  431.0 100.0 %copy-start.53 = (f32[128]{0:T(128)S(1)}, f32[128]{0:T(128)}, u32[]{:S(2)}) copy-start(f32[128]{0:T(128)} %copy-done.52) | copy-start | bytes 1540
  431.0 100.0 %copy-start.59 = (f32[128]{0:T(128)S(1)}, f32[128]{0:T(128)}, u32[]{:S(2)}) copy-start(f32[128]{0:T(128)} %copy-done.58) | copy-start | bytes 1540
  431.0 102.2 %copy-start.65 = (f32[128]{0:T(128)S(1)}, f32[128]{0:T(128)}, u32[]{:S(2)}) copy-start(f32[128]{0:T(128)} %copy-done.64) | copy-start | bytes 1540
  431.0 188.0 %copy-start.51 = (f32[2048]{0:T(1024)S(1)}, f32[2048]{0:T(1024)}, u32[]{:S(2)}) copy-start(f32[2048]{0:T(1024)} %param.29) | copy-start | bytes 24580
  431.1 190.5 %copy-start.15 = (bf16[128,1,2048]{2,0,1:T(8,128)(2,1)S(1)}, bf16[128,1,2048]{2,0,1:T(8,128)(2,1)}, u32[]{:S(2)}) copy-start(bf16[128,1,2048]{2,0,1:T(8,128)(2,1)} %get-tuple-element.119) | copy-start | bytes 1572868
  431.1 191.9 %copy-start.67 = (s32[8]{0:T(128)S(1)}, s32[8]{0:T(128)}, u32[]{:S(2)}) copy-start(s32[8]{0:T(128)} %param.17) | copy-start | bytes 100
  431.1 194.6 %copy-start.71 = (f32[512]{0:T(512)S(1)}, f32[512]{0:T(512)}, u32[]{:S(2)}) copy-start(f32[512]{0:T(512)} %param.27) | copy-start | bytes 6148
  431.1 261.8 %all-gather.11.cloned.1.call-start = ((), (), s32[]{:S(2)}) async-start(), calls=%async_computation.15 | async-start | bytes 8912896 | tf_op jit(solution)/shard_map/all_gather | solution.py:230
  621.6 15.5 copy-start.14
  621.6 15.5 copy-start.60
  622.7 227.9 %reduce-scatter.26.cloned.1.call-start = ((), (), s32[]{:S(2)}) async-start(), calls=%async_computation.20 | async-start | bytes 2359296 | tf_op jit(solution)/shard_map/reduce_scatter | solution.py:277
  625.7 11.4 copy-start.48
  637.1 215.3 %reduce-scatter.24.cloned.1.call-start = ((), (), s32[]{:S(2)}) async-start(), calls=%async_computation.19 | async-start | bytes 2359296 | tf_op jit(solution)/shard_map/reduce_scatter | solution.py:274
  637.1 4.9 copy-start.5
  637.1 4.9 copy-start.49
  641.4 76.1 %copy-start.39 = (f32[512]{0:T(512)}, f32[512]{0:T(512)S(1)}, u32[]{:S(2)}) copy-start(f32[512]{0:T(512)S(1)} %get-tuple-element.150) | copy-start | bytes 6148
  641.4 80.6 %copy-start.37 = (f32[512]{0:T(512)}, f32[512]{0:T(512)S(1)}, u32[]{:S(2)}) copy-start(f32[512]{0:T(512)S(1)} %get-tuple-element.149) | copy-start | bytes 6148
  644.2 77.9 %copy-start.41 = (f32[512]{0:T(512)}, f32[512]{0:T(512)S(1)}, u32[]{:S(2)}) copy-start(f32[512]{0:T(512)S(1)} %get-tuple-element.151) | copy-start | bytes 6148
  644.2 77.9 %copy-start.43 = (f32[512]{0:T(512)}, f32[512]{0:T(512)S(1)}, u32[]{:S(2)}) copy-start(f32[512]{0:T(512)S(1)} %get-tuple-element.152) | copy-start | bytes 6148
  645.5 47.4 %copy-start.24 = (bf16[1,128,2048]{2,1,0:T(8,128)(2,1)S(1)}, bf16[1,128,2048]{2,1,0:T(8,128)(2,1)}, u32[]{:S(2)}) copy-start(bf16[1,128,2048]{2,1,0:T(8,128)(2,1)} %param.22) | copy-start | bytes 1572868
  655.2 200.2 %reduce-scatter.22.cloned.1.call-start = ((), (), s32[]{:S(2)}) async-start(), calls=%async_computation.18 | async-start | bytes 589824 | tf_op jit(solution)/shard_map/reduce_scatter | solution.py:271
  692.9 14.3 copy-start.8
  698.8 8.4 copy-start.21
  698.8 8.4 copy-start.6
  701.7 5.6 copy-start.2
  701.7 6.3 copy-start.4
  701.7 6.3 copy-start.34
  701.7 6.3 copy-start.36
  731.6 5.4 copy-start.13
  731.6 6.8 copy-start.11
  733.7 6.1 copy-start.18
  745.4 4.5 slice-start
  752.4 150.2 %reduce-scatter.20.cloned.1.call-start = ((), (), s32[]{:S(2)}) async-start(), calls=%async_computation.17 | async-start | bytes 1769472 | tf_op jit(solution)/shard_map/reduce_scatter | solution.py:268
  763.6 231.1 %reduce-scatter.18.cloned.1.call-start = ((), (), s32[]{:S(2)}) async-start(), calls=%async_computation.16 | async-start | bytes 8912896 | tf_op jit(solution)/shard_map/reduce_scatter | solution.py:250
  773.3 221.4 %copy-start.9 = (bf16[128,1,2048]{2,0,1:T(8,128)(2,1)S(1)}, bf16[128,1,2048]{2,0,1:T(8,128)(2,1)}, u32[]{:S(2)}) copy-start(bf16[128,1,2048]{2,0,1:T(8,128)(2,1)} %param.15) | copy-start | bytes 1572868
  773.3 221.4 %copy-start.28 = (f32[2048]{0:T(1024)S(1)}, f32[2048]{0:T(1024)}, u32[]{:S(2)}) copy-start(f32[2048]{0:T(1024)} %param.18) | copy-start | bytes 24580
  773.3 221.4 %copy-start.46 = (f32[128]{0:T(128)S(1)}, f32[128]{0:T(128)}, u32[]{:S(2)}) copy-start(f32[128]{0:T(128)} %copy-done.45) | copy-start | bytes 1540
  773.3 222.8 %copy-start.69 = (f32[128]{0:T(128)S(1)}, f32[128]{0:T(128)}, u32[]{:S(2)}) copy-start(f32[128]{0:T(128)} %copy-done.68) | copy-start | bytes 1540
  773.3 222.8 %copy-start.55 = (f32[128]{0:T(128)S(1)}, f32[128]{0:T(128)}, u32[]{:S(2)}) copy-start(f32[128]{0:T(128)} %copy-done.54) | copy-start | bytes 1540
  773.3 224.4 %copy-start.30 = (f32[2048]{0:T(1024)S(1)}, f32[2048]{0:T(1024)}, u32[]{:S(2)}) copy-start(f32[2048]{0:T(1024)} %get-tuple-element.118) | copy-start | bytes 24580
  773.3 224.4 %copy-start.31 = (f32[2048]{0:T(1024)S(1)}, f32[2048]{0:T(1024)}, u32[]{:S(2)}) copy-start(f32[2048]{0:T(1024)} %get-tuple-element.107) | copy-start | bytes 24580
  773.4 224.4 %copy-start.32 = (f32[2048]{0:T(1024)S(1)}, f32[2048]{0:T(1024)}, u32[]{:S(2)}) copy-start(f32[2048]{0:T(1024)} %get-tuple-element.111) | copy-start | bytes 24580
  773.4 225.9 %copy-start.16 = (bf16[128,1,2048]{2,0,1:T(8,128)(2,1)S(1)}, bf16[128,1,2048]{2,0,1:T(8,128)(2,1)}, u32[]{:S(2)}) copy-start(bf16[128,1,2048]{2,0,1:T(8,128)(2,1)} %get-tuple-element.119) | copy-start | bytes 1572868
  773.4 225.9 %copy-start.61 = (f32[128]{0:T(128)S(1)}, f32[128]{0:T(128)}, u32[]{:S(2)}) copy-start(f32[128]{0:T(128)} %copy-done.60) | copy-start | bytes 1540
  773.4 937.6 %reduce-scatter.28.cloned.1.call-start = ((), (), s32[]{:S(2)}) async-start(), calls=%async_computation.21 | async-start | bytes 1056768
  855.4 861.5 %copy-start.1 = (bf16[512,2048]{1,0:T(8,128)(2,1)S(1)}, bf16[512,2048]{1,0:T(8,128)(2,1)}, u32[]{:S(2)}) copy-start(bf16[512,2048]{1,0:T(8,128)(2,1)} %param.28) | copy-start | bytes 6291460
  (25 other events, 46.6 us)
Sparse Core Ops, SparseCore 0:
  12.9 71.8 all-gather.4
  140.5 110.1 reduce-scatter.11
  255.5 70.2 all-gather.6
  328.3 70.3 all-gather.8
  420.8 110.1 reduce-scatter.15
  534.3 84.6 reduce-scatter.13
  622.8 70.0 all-gather.10
  695.3 56.2 reduce-scatter.25
  754.1 60.7 reduce-scatter.23
  817.0 38.2 reduce-scatter.21
  857.9 44.5 reduce-scatter.19
  906.2 88.4 reduce-scatter.17
  999.3 711.5 reduce-scatter.27
where the time goes:
time: 1730 us; the launch traced here: 1720 us
  waiting for transfers between devices  1380 us (80%)
  matrix products  158 us (9%)
  blocking collectives  75.9 us (4%)
  other arithmetic  57.2 us (3%)
  local copies, waits for them, and re-layouts  22.4 us (1%)
    unnamed x14, waiting for transfers between devices  709 us
    reduce_scatter x1, waiting for transfers between devices, shards(): lax.psum_scatter(jnp.einsum('rse,ed->rsd', piece, out_weight, preferred_e...  110 us
    reduce_scatter x1, waiting for transfers between devices, shards(): lax.psum_scatter(jnp.einsum('rsf,df->rsd', piece, w_in, preferred_element...  99.9 us
    reduce_scatter x1, waiting for transfers between devices, shards(): lax.psum_scatter(jnp.einsum('rsc,dc->rsd', piece, joint_weight, preferred...  90.2 us
    reduce_scatter x1, waiting for transfers between devices, shards(): lax.psum_scatter(jnp.einsum('rsf,fd->rsd', piece, w_out, preferred_elemen...  85.7 us
    unnamed x1, blocking collectives  75.9 us
    all_gather x1, waiting for transfers between devices, shards(): normed_full = lax.all_gather(normed_low, 'tensor', axis=0, tiled=True)  68.1 us
    all_gather x1, waiting for transfers between devices, shards(): second_full = lax.all_gather(second_low, 'tensor', axis=0, tiled=True)  67 us
  transfers between devices with their start and end apart: 13, of which 11 were waited for; matrix products, arithmetic and copies ran while one was open for 9% of the time, Pallas kernels for 0%

commit v1 on v0

--- a/solution.py
+++ b/solution.py
@@ -129,7 +129,13 @@
     )
     inputs = tokens.astype(jnp.float32)
     normed_low = layer_norm(inputs, ln1_gain, ln1_bias).astype(jnp.bfloat16)
-    normed_full = lax.all_gather(normed_low, "tensor", axis=0, tiled=True)
+    lanes = []
+    count_all = lax.axis_size("tensor")
+    for no in range(normed_low.ndim):
+        lanes.append(count_all if no == 0 else 1)
+    normed_full = lax.all_to_all(
+        jnp.tile(normed_low, lanes), tiled=True, split_axis=0, axis_name="tensor", concat_axis=0
+    )
     joint_weight = w_qkv.reshape(model_width, 3 * local_width)
     projected = jnp.dot(
         normed_full.reshape(seq_total * seq_count, model_width),

time: 1730 us -> 1870 us (1.081)
  local copies, waits for them, and re-layouts: 22.4 us -> 98 us
  waiting for transfers between devices: 1380 us -> 1410 us
    all_to_all x0 -> x1, waiting for transfers between devices: none -> 143 us  [shards(): lax.all_to_all(jnp.tile(normed_low, lanes), tiled=True, split_axis=0, axi...]
    all_gather x1 -> x0, waiting for transfers between devices: 68.1 us -> none  [shards(): normed_full = lax.all_gather(normed_low, 'tensor', axis=0, tiled=True)]
    reshape x0 -> x1, local copies, waits for them, and re-layouts: none -> 39.2 us  [shards(): normed_full.reshape(seq_total * seq_count, model_width)]
    all_gather x1, waiting for transfers between devices: 37.3 us -> 0.02 us  [shards(): piece = lax.all_gather(branch_low, 'tensor', axis=0, tiled=True)]
    unnamed x163 -> x165, local copies, waits for them, and re-layouts: 17.5 us -> 49 us
    unnamed x14 -> x13, waiting for transfers between devices: 709 us -> 707 us
  transfers between devices with their start and end apart: 13 -> 13, of which waited for: 11 -> 10; matrix products, arithmetic and copies ran while one was open for 9% -> 10% of each run, Pallas kernels for 0% -> 0%
where the time goes in v1:
time: 1870 us; the launch traced here: 1860 us
  waiting for transfers between devices  1410 us (75%)
  matrix products  163 us (9%)
  local copies, waits for them, and re-layouts  98 us (5%)
  blocking collectives  73.7 us (4%)
  other arithmetic  69.1 us (4%)
    unnamed x13, waiting for transfers between devices  707 us
    all_to_all x1, waiting for transfers between devices, shards(): lax.all_to_all(jnp.tile(normed_low, lanes), tiled=True, split_axis=0, axi...  143 us
    reduce_scatter x1, waiting for transfers between devices, shards(): lax.psum_scatter(jnp.einsum('rse,ed->rsd', piece, out_weight, preferred_e...  113 us
    reduce_scatter x1, waiting for transfers between devices, shards(): lax.psum_scatter(jnp.einsum('rsf,df->rsd', piece, w_in, preferred_element...  99.9 us
    reduce_scatter x1, waiting for transfers between devices, shards(): lax.psum_scatter(jnp.einsum('rsc,dc->rsd', piece, joint_weight, preferred...  89.8 us
    reduce_scatter x1, waiting for transfers between devices, shards(): lax.psum_scatter(jnp.einsum('rsf,fd->rsd', piece, w_out, preferred_elemen...  85.8 us
    unnamed x1, blocking collectives  73.7 us
    all_gather x1, waiting for transfers between devices, shards(): second_full = lax.all_gather(second_low, 'tensor', axis=0, tiled=True)  67 us
  transfers between devices with their start and end apart: 13, of which 10 were waited for; matrix products, arithmetic and copies ran while one was open for 10% of the time, Pallas kernels for 0%

profile of v1, /device:TPU:96, one launch (start us, length us, event | category | flops | bytes accessed | tf_op | source)
XLA Modules:
  0.0 1859.6 jit_solution(11648446915370937903)
XLA Ops:
  10.9 1.5 fusion.91
  12.4 4.3 tile.12
  17.2 12.4 reduce.12
  29.6 14.5 reshape.500
  44.1 7.2 all-to-all-start
  51.6 2.7 copy.64
  55.5 143.5 %all-to-all-done = bf16[16,2,131072]{2,1,0:T(2,128)(2,1)} async-done(((bf16[16,2,131072]{2,1,0:T(2,128)(2,1)}), bf16[16,2,131072]{2,1,0:T(2,128)(2,1)}, u32[]{:S(2)}, u32[]{:S(2)}) %all-to-all-start) | async-done | bytes 8388640 | tf_op jit(solution)/shard_map/all_to_all | solution.py:136
  199.0 16.3 reshape.501
  215.3 12.2 fusion.32
  228.8 3.5 fusion.115
  232.4 3.9 fusion.118
  236.2 4.0 online-softmax.3
  241.2 5.2 fusion.117
  246.4 4.0 online-softmax.2
  251.3 5.1 fusion.116
  256.4 4.0 online-softmax.1
  261.5 4.2 online-softmax
  267.3 8.1 convolution_bitcast_fusion.1
  275.4 113.2 %reduce-scatter.12.cloned.1.call-done = f32[128,1,2048]{2,0,1:T(8,128)} async-done(((f32[2048,1,2048]{2,0,1:T(8,128)}), f32[128,1,2048]{2,0,1:T(8,128)}) %reduce-scatter.12.cloned.1.call-update) | async-done | bytes 1048592 | tf_op jit(solution)/shard_map/reduce_scatter | solution.py:172
  388.6 1.6 fusion.113
  391.5 1.7 add_convert_fusion.3
  393.9 2.6 convert_reduce_fusion.4
  396.6 67.0 %all-gather.4.cloned.1.call-done = bf16[2048,1,2048]{2,0,1:T(8,128)(2,1)} async-done(((bf16[128,1,2048]{2,0,1:T(8,128)(2,1)}), bf16[2048,1,2048]{2,0,1:T(8,128)(2,1)}) %all-gather.4.cloned.1.call-update) | async-done | bytes 8388624 | tf_op jit(solution)/shard_map/all_gather | solution.py:182
  463.6 10.5 fusion.15
  474.1 62.6 %all-gather.6.cloned.1.call-done = bf16[2048,1,2048]{2,0,1:T(8,128)(2,1)} async-done(((bf16[128,1,2048]{2,0,1:T(8,128)(2,1)}), bf16[2048,1,2048]{2,0,1:T(8,128)(2,1)}) %all-gather.6.cloned.1.call-update) | async-done | bytes 8388624 | tf_op jit(solution)/shard_map/all_gather | solution.py:208
  536.7 12.7 convert_reduce_fusion
  550.8 8.2 convolution_bitcast_fusion
  559.1 10.3 convert_bitcast_fusion.1
  569.5 99.9 %reduce-scatter.16.cloned.1.call-done = f32[128,1,2048]{2,0,1:T(8,128)} async-done(((f32[2048,1,2048]{2,0,1:T(8,128)}), f32[128,1,2048]{2,0,1:T(8,128)}) %reduce-scatter.16.cloned.1.call-update) | async-done | bytes 1048592 | tf_op jit(solution)/shard_map/reduce_scatter | solution.py:224
  669.4 2.2 multiply_reduce_fusion.4
  671.6 85.8 %reduce-scatter.14.cloned.1.call-done = bf16[128,1,2048]{2,0,1:T(8,128)(2,1)} async-done(((bf16[2048,1,2048]{2,0,1:T(8,128)(2,1)}), bf16[128,1,2048]{2,0,1:T(8,128)(2,1)}) %reduce-scatter.14.cloned.1.call-update) | async-done | bytes 524304 | tf_op jit(solution)/shard_map/reduce_scatter | solution.py:194
  757.4 2.5 fusion.112
  764.1 11.2 multiply_convert_fusion
  775.4 39.2 %copy.85 = bf16[2048,1,2048]{0,2,1:T(8,128)(2,1)} copy(bf16[2048,1,2048]{2,1,0:T(2,128)(2,1)} %reshape.501) | data formatting | bytes 16777216 | tf_op jit(solution)/shard_map/reshape | solution.py:141
  814.6 3.2 exponential_reduce_fusion
  823.1 9.6 multiply_convert_fusion.1
  833.0 5.9 fusion.46
  838.9 2.9 fusion.99
  841.8 2.8 fusion.102
  844.7 2.7 fusion.105
  848.3 9.5 multiply_reduce_fusion
  857.8 4.6 multiply_convert_fusion.3
  862.4 9.7 multiply_convert_fusion.2
  872.1 2.1 fusion.76
  874.2 3.3 fusion.78
  878.9 1.4 fusion.77
  884.2 1.7 convolution_add_fusion.2
  886.0 1.7 convolution_add_fusion.1
  887.7 2.8 fusion.57
  890.5 2.3 fusion.54
  894.0 1.7 copy.73
  895.7 8.3 fusion.39
  904.1 9.8 convert_bitcast_fusion
  914.8 73.7 %all-reduce = f32[8192]{0:T(1024)S(1)} all-reduce(f32[8192]{0:T(1024)S(1)} %broadcast_multiply_fusion.1), channel_id=10, replica_groups=mesh['group'=4,'dp'=2,'tensor'=16] {'group','dp','tensor'}, use_global_device_ids=true, to_apply=%region_38.39.clone | all-reduce | flops 8192 | bytes 65536
  989.1 1.8 convert_element_type.264
  990.9 1.8 convert_element_type.261
  993.1 1.7 convert_element_type.259
  994.8 45.6 %reduce-scatter.20.cloned.1.call-done = bf16[256,3,1,128]{3,0,1,2:T(8,128)(2,1)} async-done(((bf16[2048,3,1,128]{3,0,1,2:T(8,128)(2,1)}), bf16[256,3,1,128]{3,0,1,2:T(8,128)(2,1)}) %reduce-scatter.20.cloned.1.call-update) | async-done | bytes 196624 | tf_op jit(solution)/shard_map/reduce_scatter | solution.py:274
  1040.4 2.0 copy.75
  1042.3 89.8 %reduce-scatter.18.cloned.1.call-done = bf16[128,1,2048]{2,0,1:T(8,128)(2,1)} async-done(((bf16[2048,1,2048]{2,0,1:T(8,128)(2,1)}), bf16[128,1,2048]{2,0,1:T(8,128)(2,1)}) %reduce-scatter.18.cloned.1.call-update) | async-done | bytes 524304 | tf_op jit(solution)/shard_map/reduce_scatter | solution.py:256
  1132.2 1.4 convert_reduce_fusion.2
  1133.6 1.6 fusion.84
  1136.7 2.7 add_convert_fusion
  1139.4 707.3 %reduce-scatter.28.cloned.1.call-done = f32[16,8]{1,0:T(8,128)} async-done(((f32[2048,8]{1,0:T(8,128)}), f32[16,8]{1,0:T(8,128)}) %reduce-scatter.28.cloned.1.call-update) | async-done | bytes 528
  (244 shorter events, 40.2 us)
Async XLA Ops:
  7.2 529.5 %copy-start = (bf16[512,2048]{1,0:T(8,128)(2,1)S(1)}, bf16[512,2048]{1,0:T(8,128)(2,1)}, u32[]{:S(2)}) copy-start(bf16[512,2048]{1,0:T(8,128)(2,1)} %param.28) | copy-start | bytes 6291460
  44.1 10.1 copy-start.66
  44.1 11.4 copy-start.63
  44.1 154.9 %all-to-all-start = ((bf16[16,2,131072]{2,1,0:T(2,128)(2,1)}), bf16[16,2,131072]{2,1,0:T(2,128)(2,1)}, u32[]{:S(2)}, u32[]{:S(2)}) async-start(bf16[16,2,131072]{2,1,0:T(2,128)(2,1)} %reshape.500), calls=%async_computation | async-start | bytes 16777216 | tf_op jit(solution)/shard_map/all_to_all | solution.py:136
  51.3 337.2 %reduce-scatter.12.cloned.1.call-start = ((), (), s32[]{:S(2)}) async-start(), calls=%async_computation.10 | async-start | bytes 17825792 | tf_op jit(solution)/shard_map/reduce_scatter | solution.py:172
  54.8 196.5 %copy-start.35 = (s32[512]{0:T(512)}, s32[512]{0:T(512)S(1)}, u32[]{:S(2)}) copy-start(s32[512]{0:T(512)S(1)} %iota_add_fusion.2) | copy-start | bytes 6148
  54.8 186.3 %copy-start.33 = (s32[512]{0:T(512)}, s32[512]{0:T(512)S(1)}, u32[]{:S(2)}) copy-start(s32[512]{0:T(512)S(1)} %iota_add_fusion.1) | copy-start | bytes 6148
  55.5 172.1 %copy-start.56 = (f32[128]{0:T(128)}, f32[128]{0:T(128)S(1)}, u32[]{:S(2)}) copy-start(f32[128]{0:T(128)S(1)} %get-tuple-element.150) | copy-start | bytes 1540
  227.6 4.8 copy-start.12
  227.6 23.7 %copy-start.17 = (bf16[2048,1,128]{2,0,1:T(8,128)(2,1)}, bf16[2048,1,128]{2,0,1:T(8,128)(2,1)S(1)}, u32[]{:S(2)}) copy-start(bf16[2048,1,128]{2,0,1:T(8,128)(2,1)S(1)} %fusion.86) | copy-start | bytes 1572868
  260.4 6.8 copy-start.23
  275.3 116.1 %copy-start.29 = (f32[2048]{0:T(1024)S(1)}, f32[2048]{0:T(1024)}, u32[]{:S(2)}) copy-start(f32[2048]{0:T(1024)} %param.24) | copy-start | bytes 24580
  275.4 188.3 %all-gather.4.cloned.1.call-start = ((), (), s32[]{:S(2)}) async-start(), calls=%async_computation.11 | async-start | bytes 8912896 | tf_op jit(solution)/shard_map/all_gather | solution.py:182
  393.2 143.5 %all-gather.6.cloned.1.call-start = ((), (), s32[]{:S(2)}) async-start(), calls=%async_computation.13 | async-start | bytes 8912896 | tf_op jit(solution)/shard_map/all_gather | solution.py:208
  396.6 272.8 %reduce-scatter.16.cloned.1.call-start = ((), (), s32[]{:S(2)}) async-start(), calls=%async_computation.14 | async-start | bytes 17825792 | tf_op jit(solution)/shard_map/reduce_scatter | solution.py:224
  536.7 14.0 copy-start.70
  559.0 198.4 %reduce-scatter.14.cloned.1.call-start = ((), (), s32[]{:S(2)}) async-start(), calls=%async_computation.12 | async-start | bytes 8912896 | tf_op jit(solution)/shard_map/reduce_scatter | solution.py:194
  569.3 100.0 %copy-start.53 = (f32[128]{0:T(128)S(1)}, f32[128]{0:T(128)}, u32[]{:S(2)}) copy-start(f32[128]{0:T(128)} %copy-done.52) | copy-start | bytes 1540
  569.3 100.0 %copy-start.59 = (f32[128]{0:T(128)S(1)}, f32[128]{0:T(128)}, u32[]{:S(2)}) copy-start(f32[128]{0:T(128)} %copy-done.58) | copy-start | bytes 1540
  569.3 102.3 %copy-start.65 = (f32[128]{0:T(128)S(1)}, f32[128]{0:T(128)}, u32[]{:S(2)}) copy-start(f32[128]{0:T(128)} %copy-done.64) | copy-start | bytes 1540
  569.3 188.1 %copy-start.51 = (f32[2048]{0:T(1024)S(1)}, f32[2048]{0:T(1024)}, u32[]{:S(2)}) copy-start(f32[2048]{0:T(1024)} %param.29) | copy-start | bytes 24580
  569.4 190.6 %copy-start.15 = (bf16[128,1,2048]{2,0,1:T(8,128)(2,1)S(1)}, bf16[128,1,2048]{2,0,1:T(8,128)(2,1)}, u32[]{:S(2)}) copy-start(bf16[128,1,2048]{2,0,1:T(8,128)(2,1)} %get-tuple-element.133) | copy-start | bytes 1572868
  569.4 192.0 %copy-start.67 = (s32[8]{0:T(128)S(1)}, s32[8]{0:T(128)}, u32[]{:S(2)}) copy-start(s32[8]{0:T(128)} %param.17) | copy-start | bytes 100
  569.4 194.7 %copy-start.71 = (f32[512]{0:T(512)S(1)}, f32[512]{0:T(512)}, u32[]{:S(2)}) copy-start(f32[512]{0:T(512)} %param.27) | copy-start | bytes 6148
  569.4 263.6 %all-gather.8.cloned.1.call-start = ((), (), s32[]{:S(2)}) async-start(), calls=%async_computation.15 | async-start | bytes 8912896 | tf_op jit(solution)/shard_map/all_gather | solution.py:236
  760.0 15.4 copy-start.14
  760.0 15.4 copy-start.60
  761.1 228.0 %reduce-scatter.26.cloned.1.call-start = ((), (), s32[]{:S(2)}) async-start(), calls=%async_computation.20 | async-start | bytes 2359296 | tf_op jit(solution)/shard_map/reduce_scatter | solution.py:283
  775.4 39.2 %copy-start.48 = (f32[512]{0:T(512)S(1)}, f32[512]{0:T(512)}, u32[]{:S(2)}) copy-start(f32[512]{0:T(512)} %get-tuple-element.158) | copy-start | bytes 6148
  775.4 215.5 %reduce-scatter.24.cloned.1.call-start = ((), (), s32[]{:S(2)}) async-start(), calls=%async_computation.19 | async-start | bytes 2359296 | tf_op jit(solution)/shard_map/reduce_scatter | solution.py:280
  814.6 3.6 copy-start.50
  814.6 5.0 copy-start.5
  814.6 5.0 copy-start.49
  818.9 38.9 %copy-start.39 = (f32[512]{0:T(512)}, f32[512]{0:T(512)S(1)}, u32[]{:S(2)}) copy-start(f32[512]{0:T(512)S(1)} %get-tuple-element.164) | copy-start | bytes 6148
  818.9 43.5 %copy-start.37 = (f32[512]{0:T(512)}, f32[512]{0:T(512)S(1)}, u32[]{:S(2)}) copy-start(f32[512]{0:T(512)S(1)} %get-tuple-element.163) | copy-start | bytes 6148
  821.8 40.6 %copy-start.41 = (f32[512]{0:T(512)}, f32[512]{0:T(512)S(1)}, u32[]{:S(2)}) copy-start(f32[512]{0:T(512)S(1)} %get-tuple-element.165) | copy-start | bytes 6148
  821.8 40.6 %copy-start.43 = (f32[512]{0:T(512)}, f32[512]{0:T(512)S(1)}, u32[]{:S(2)}) copy-start(f32[512]{0:T(512)S(1)} %get-tuple-element.166) | copy-start | bytes 6148
  823.1 9.9 copy-start.24
  832.7 160.4 %reduce-scatter.22.cloned.1.call-start = ((), (), s32[]{:S(2)}) async-start(), calls=%async_computation.18 | async-start | bytes 589824 | tf_op jit(solution)/shard_map/reduce_scatter | solution.py:277
  833.0 14.4 copy-start.8
  838.9 8.5 copy-start.21
  838.9 8.5 copy-start.6
  841.8 5.6 copy-start.2
  841.8 6.5 copy-start.4
  841.8 6.5 copy-start.34
  841.8 6.5 copy-start.36
  872.1 5.4 copy-start.13
  872.1 6.8 copy-start.11
  874.2 6.0 copy-start.18
  885.9 4.5 slice-start
  892.8 147.6 %reduce-scatter.20.cloned.1.call-start = ((), (), s32[]{:S(2)}) async-start(), calls=%async_computation.17 | async-start | bytes 1769472 | tf_op jit(solution)/shard_map/reduce_scatter | solution.py:274
  904.0 228.1 %reduce-scatter.18.cloned.1.call-start = ((), (), s32[]{:S(2)}) async-start(), calls=%async_computation.16 | async-start | bytes 8912896 | tf_op jit(solution)/shard_map/reduce_scatter | solution.py:256
  913.9 218.2 %copy-start.9 = (bf16[128,1,2048]{2,0,1:T(8,128)(2,1)S(1)}, bf16[128,1,2048]{2,0,1:T(8,128)(2,1)}, u32[]{:S(2)}) copy-start(bf16[128,1,2048]{2,0,1:T(8,128)(2,1)} %param.15) | copy-start | bytes 1572868
  913.9 218.2 %copy-start.28 = (f32[2048]{0:T(1024)S(1)}, f32[2048]{0:T(1024)}, u32[]{:S(2)}) copy-start(f32[2048]{0:T(1024)} %param.18) | copy-start | bytes 24580
  913.9 218.2 %copy-start.46 = (f32[128]{0:T(128)S(1)}, f32[128]{0:T(128)}, u32[]{:S(2)}) copy-start(f32[128]{0:T(128)} %copy-done.45) | copy-start | bytes 1540
  914.0 219.6 %copy-start.69 = (f32[128]{0:T(128)S(1)}, f32[128]{0:T(128)}, u32[]{:S(2)}) copy-start(f32[128]{0:T(128)} %copy-done.68) | copy-start | bytes 1540
  914.0 219.6 %copy-start.55 = (f32[128]{0:T(128)S(1)}, f32[128]{0:T(128)}, u32[]{:S(2)}) copy-start(f32[128]{0:T(128)} %copy-done.54) | copy-start | bytes 1540
  914.0 221.2 %copy-start.30 = (f32[2048]{0:T(1024)S(1)}, f32[2048]{0:T(1024)}, u32[]{:S(2)}) copy-start(f32[2048]{0:T(1024)} %get-tuple-element.132) | copy-start | bytes 24580
  914.0 221.2 %copy-start.31 = (f32[2048]{0:T(1024)S(1)}, f32[2048]{0:T(1024)}, u32[]{:S(2)}) copy-start(f32[2048]{0:T(1024)} %get-tuple-element.121) | copy-start | bytes 24580
  914.0 221.2 %copy-start.32 = (f32[2048]{0:T(1024)S(1)}, f32[2048]{0:T(1024)}, u32[]{:S(2)}) copy-start(f32[2048]{0:T(1024)} %get-tuple-element.125) | copy-start | bytes 24580
  914.0 222.7 %copy-start.16 = (bf16[128,1,2048]{2,0,1:T(8,128)(2,1)S(1)}, bf16[128,1,2048]{2,0,1:T(8,128)(2,1)}, u32[]{:S(2)}) copy-start(bf16[128,1,2048]{2,0,1:T(8,128)(2,1)} %get-tuple-element.133) | copy-start | bytes 1572868
  914.0 222.7 %copy-start.61 = (f32[128]{0:T(128)S(1)}, f32[128]{0:T(128)}, u32[]{:S(2)}) copy-start(f32[128]{0:T(128)} %copy-done.60) | copy-start | bytes 1540
  914.0 932.7 %reduce-scatter.28.cloned.1.call-start = ((), (), s32[]{:S(2)}) async-start(), calls=%async_computation.21 | async-start | bytes 1056768
  993.1 859.5 %copy-start.1 = (bf16[512,2048]{1,0:T(8,128)(2,1)S(1)}, bf16[512,2048]{1,0:T(8,128)(2,1)}, u32[]{:S(2)}) copy-start(bf16[512,2048]{1,0:T(8,128)(2,1)} %param.28) | copy-start | bytes 6291460
  (25 other events, 44.4 us)
Sparse Core Ops, SparseCore 0:
  275.5 113.0 reduce-scatter.11
  393.3 70.2 all-gather.3
  466.4 70.3 all-gather.5
  559.1 110.1 reduce-scatter.15
  672.6 84.7 reduce-scatter.13
  761.2 69.9 all-gather.7
  833.7 56.8 reduce-scatter.25
  892.9 59.3 reduce-scatter.23
  954.7 38.4 reduce-scatter.21
  995.5 44.7 reduce-scatter.19
  1044.2 87.9 reduce-scatter.17
  1136.8 709.8 reduce-scatter.27
